TPU v7x, 32 devices: a whole 2x2x4 slice. The times are simulated.
32 devices in a mesh: mp: 2 (over x), dp: 16 (over z, y, core).
Axes of the slice: x: 2, y: 2, z: 4, core: 2. Of those that a mesh axis runs over, the one named last changes fastest.
Arguments:
- image: bfloat16 [16, 128, 1024], P('dp', 'mp'), may hold values from -8 to 8
- text: bfloat16 [2048, 1024], P('dp'), may hold values from -8 to 8
- logit_scale: float32 [1], replicated, may hold values from 10 to 30
Outputs:
- row_loss: float32 [16, 128], P('dp', 'mp')
- col_loss: float32 [16, 128], P('dp', 'mp')
All inputs are finite; a program needn't handle non-finite values.
Results may differ from a plain program's by a relative error of at most 0.012.
Values may be sent and summed in bfloat16 or wider, within the bound.
A program may use at most 128 MiB of HBM per device.

v0:
```python
import jax
import jax.numpy as jnp
from jax import lax
from jax.sharding import PartitionSpec as P


def swapped(array, axis, stride):
    return lax.ppermute(array, axis, [(i, i ^ 1 << stride) for i in range(lax.axis_size(axis))])


def normalize(rows):
    wide = rows.astype(jnp.float32)
    return (wide * lax.rsqrt(jnp.sum(wide * wide, axis=1, keepdims=True) + 1e-06)).astype(
        jnp.bfloat16
    )


def bit_of(index, bit):
    return index // (1 << bit) % 2


def join_pair(mine, other, upper):
    return jnp.where(
        upper == 1, jnp.concatenate([other, mine], axis=0), jnp.concatenate([mine, other], axis=0)
    )


def on_device(image, text, logit_scale):
    scale = logit_scale[0]
    own_img = normalize(image[0])
    half = own_img.shape[0]
    text_n = normalize(text)
    group = lax.axis_index("mp")
    own_text = lax.dynamic_slice_in_dim(text_n, group * half, half, 0)
    diag = scale * jnp.sum(own_img.astype(jnp.float32) * own_text.astype(jnp.float32), axis=1)
    place = lax.axis_index("dp")
    levels = lax.axis_size("dp").bit_length() - 1
    image_rows = lax.all_gather(own_img, "mp", axis=0, tiled=True)
    for bit in range(3):
        partner = swapped(image_rows, "dp", bit)
        image_rows = join_pair(image_rows, partner, bit_of(place, bit))
    text_cols = own_text
    for bit in range(3, levels):
        partner = swapped(text_cols, "dp", bit)
        text_cols = join_pair(text_cols, partner, bit_of(place, bit))
    scores = scale * jnp.einsum(
        "hd,cd->hc", image_rows, text_cols, preferred_element_type=jnp.float32
    )
    weights = jnp.exp(scores)
    row_buffer = jnp.sum(weights, axis=1)
    col_buffer = jnp.sum(weights, axis=0)
    for bit in (2, 1, 0):
        count = row_buffer.shape[0] // 2
        upper = bit_of(place, bit)
        keep = jnp.where(upper == 1, row_buffer[count:], row_buffer[:count])
        leave = jnp.where(upper == 1, row_buffer[:count], row_buffer[count:])
        row_buffer = keep + swapped(leave, "dp", bit)
    row_total = lax.psum_scatter(row_buffer, "mp", scatter_dimension=0, tiled=True)
    for bit in reversed(range(3, levels)):
        count = col_buffer.shape[0] // 2
        upper = bit_of(place, bit)
        keep = jnp.where(upper == 1, col_buffer[count:], col_buffer[:count])
        leave = jnp.where(upper == 1, col_buffer[:count], col_buffer[count:])
        col_buffer = keep + swapped(leave, "dp", bit)
    row_loss = (jnp.log(row_total) - diag).reshape(1, half)
    col_loss = (jnp.log(col_buffer) - diag).reshape(1, half)
    return (row_loss, col_loss)


def solution(mesh):
    placed = (P("dp", "mp", None), P("dp", None), P())
    return jax.shard_map(
        on_device,
        mesh=mesh,
        in_specs=placed,
        out_specs=(P("dp", "mp"), P("dp", "mp")),
        check_vma=False,
    )
```

profile of v0, /device:TPU:0, one launch (start us, length us, event | category | flops | bytes accessed | tf_op | source)
XLA Modules:
  0.0 70.3 jit_solution(10011079483060247512)
XLA Ops:
  0.6 0.0 copy-start
  0.6 1.1 %multiply_reduce_fusion = f32[128]{0:T(128)S(1)} fusion(bf16[128,1024]{1,0:T(8,128)(2,1)} %param.4), kind=kLoop, calls=%fused_computation.12 | loop fusion | flops 393088 | bytes 262656 | tf_op jit(solution)/shard_map/reduce_sum | solution.py:13
  1.8 1.0 %convert_element_type.24 = f32[128,1024]{1,0:T(8,128)S(1)} convert(bf16[128,1024]{1,0:T(8,128)(2,1)} %param.4) | non-fusion elementwise | flops 131072 | bytes 786432 | tf_op jit(solution)/shard_map/convert_element_type | solution.py:12
  2.8 0.0 copy-done
  2.8 0.1 fusion.9
  2.9 0.1 dynamic-slice.2
  3.0 0.2 multiply_reduce_fusion.1
  3.2 7.1 %all_gather.3 = bf16[128,1024]{1,0:T(8,128)(2,1)S(1)} all-gather(bf16[64,1024]{1,0:T(8,128)(2,1)S(1)} %get-tuple-element.6), channel_id=1, replica_groups=mesh['mp'=2,'dp'=16] {'mp'}, dimensions={0}, use_global_device_ids=true | all-gather | bytes 393216 | tf_op jit(solution)/shard_map/all_gather | solution.py:38
  10.3 0.0 collective-permute-start
  10.3 1.5 %collective-permute-done = bf16[128,1024]{1,0:T(8,128)(2,1)S(1)} collective-permute-done((bf16[128,1024]{1,0:T(8,128)(2,1)S(1)}, bf16[128,1024]{1,0:T(8,128)(2,1)S(1)}, u32[]{:S(2)}, u32[]{:S(2)}) %collective-permute-start) | collective-permute-done | bytes 262176 | tf_op jit(solution)/shard_map/ppermute | solution.py:8
  11.9 0.1 maximum_select_fusion.7
  12.0 1.8 %collective-permute-start.1 = (bf16[256,1024]{1,0:T(8,128)(2,1)S(1)}, bf16[256,1024]{1,0:T(8,128)(2,1)S(1)}, u32[]{:S(2)}, u32[]{:S(2)}) collective-permute-start(bf16[256,1024]{1,0:T(8,128)(2,1)S(1)} %maximum_select_fusion.7), channel_id=1, source_target_pairs={{0,2},{1,3},{2,0},{3,1},{4,6},{5,7},{6,4},{7,5},{8,10},{9,11},{10,... | collective-permute-start | bytes 1572872 | tf_op jit(solution)/shard_map/ppermute | solution.py:8
  13.9 12.2 %collective-permute-done.1 = bf16[256,1024]{1,0:T(8,128)(2,1)S(1)} collective-permute-done((bf16[256,1024]{1,0:T(8,128)(2,1)S(1)}, bf16[256,1024]{1,0:T(8,128)(2,1)S(1)}, u32[]{:S(2)}, u32[]{:S(2)}) %collective-permute-start.1) | collective-permute-done | bytes 524320 | tf_op jit(solution)/shard_map/ppermute | solution.py:8
  26.1 0.5 maximum_select_fusion.6
  26.6 1.9 %collective-permute-start.2 = (bf16[512,1024]{1,0:T(8,128)(2,1)S(1)}, bf16[512,1024]{1,0:T(8,128)(2,1)S(1)}, u32[]{:S(2)}, u32[]{:S(2)}) collective-permute-start(bf16[512,1024]{1,0:T(8,128)(2,1)S(1)} %maximum_select_fusion.6), channel_id=1, source_target_pairs={{0,4},{1,5},{2,6},{3,7},{4,0},{5,1},{6,2},{7,3},{8,12},{9,13},{10,... | collective-permute-start | bytes 3145736 | tf_op jit(solution)/shard_map/ppermute | solution.py:8
  28.4 2.6 %collective-permute-start.3 = (bf16[64,1024]{1,0:T(8,128)(2,1)S(1)}, bf16[64,1024]{1,0:T(8,128)(2,1)S(1)}, u32[]{:S(2)}, u32[]{:S(2)}) collective-permute-start(bf16[64,1024]{1,0:T(8,128)(2,1)S(1)} %get-tuple-element.5), channel_id=1, source_target_pairs={{0,8},{1,9},{2,10},{3,11},{4,12},{5,13},{6,14},{7,15},{8,0},{9,1},... | collective-permute-start | bytes 393224 | tf_op jit(solution)/shard_map/ppermute | solution.py:8
  31.7 21.4 %collective-permute-done.3 = bf16[64,1024]{1,0:T(8,128)(2,1)S(1)} collective-permute-done((bf16[64,1024]{1,0:T(8,128)(2,1)S(1)}, bf16[64,1024]{1,0:T(8,128)(2,1)S(1)}, u32[]{:S(2)}, u32[]{:S(2)}) %collective-permute-start.3) | collective-permute-done | bytes 131104 | tf_op jit(solution)/shard_map/ppermute | solution.py:8
  53.1 0.7 %collective-permute-done.2 = bf16[512,1024]{1,0:T(8,128)(2,1)S(1)} collective-permute-done((bf16[512,1024]{1,0:T(8,128)(2,1)S(1)}, bf16[512,1024]{1,0:T(8,128)(2,1)S(1)}, u32[]{:S(2)}, u32[]{:S(2)}) %collective-permute-start.2) | collective-permute-done | bytes 1048608 | tf_op jit(solution)/shard_map/ppermute | solution.py:8
  53.8 0.0 copy-start.1
  53.8 0.8 %fusion.26 = (f32[128]{0:T(128)S(1)}, f32[1024]{0:T(1024)S(1)}) fusion(bf16[64,1024]{1,0:T(8,128)(2,1)S(1)} %get-tuple-element.5, bf16[64,1024]{1,0:T(8,128)(2,1)S(1)} %collective-permute-done.3, pred[]{:T(512)S(6)} %eq.32, bf16[512,1024]{1,0:T(8,128)(2,1)S(1)} %maximum_select_fusion.6, bf16[512,1024]{1,0:T(8,128)(2,1)S(1)} %collective-permute-done.2, ...), kind=kOutput, calls=%fused_computation.46 | convolution fusion | flops 279444352 | bytes 2363910 | tf_op jit(solution)/shard_map/hd,cd->hc/dot_general | solution.py:46
  54.7 2.8 %collective-permute-start.4 = (f32[512]{0:T(512)S(1)}, f32[512]{0:T(512)S(1)}, u32[]{:S(2)}, u32[]{:S(2)}) collective-permute-start(f32[512]{0:T(512)S(1)} %slice_select_fusion), channel_id=1, source_target_pairs={{0,4},{1,5},{2,6},{3,7},{4,0},{5,1},{6,2},{7,3},{8,12},{9,13},{10,... | collective-permute-start | bytes 6152 | tf_op jit(solution)/shard_map/ppermute | solution.py:8
  57.5 1.6 %collective-permute-done.4 = f32[512]{0:T(512)S(1)} collective-permute-done((f32[512]{0:T(512)S(1)}, f32[512]{0:T(512)S(1)}, u32[]{:S(2)}, u32[]{:S(2)}) %collective-permute-start.4) | collective-permute-done | bytes 2080 | tf_op jit(solution)/shard_map/ppermute | solution.py:8
  59.1 1.6 %collective-permute-start.5 = (f32[256]{0:T(256)S(1)}, f32[256]{0:T(256)S(1)}, u32[]{:S(2)}, u32[]{:S(2)}) collective-permute-start(f32[256]{0:T(256)S(1)} %broadcast_select_fusion.2), channel_id=1, source_target_pairs={{0,2},{1,3},{2,0},{3,1},{4,6},{5,7},{6,4},{7,5},{8,10},{9,11},{10,... | collective-permute-start | bytes 3080 | tf_op jit(solution)/shard_map/ppermute | solution.py:8
  60.7 0.0 copy-done.1
  60.7 0.6 dynamic-slice
  61.9 0.8 %collective-permute-done.5 = f32[256]{0:T(256)S(1)} collective-permute-done((f32[256]{0:T(256)S(1)}, f32[256]{0:T(256)S(1)}, u32[]{:S(2)}, u32[]{:S(2)}) %collective-permute-start.5) | collective-permute-done | bytes 1056 | tf_op jit(solution)/shard_map/ppermute | solution.py:8
  62.7 0.1 collective-permute-start.6
  62.8 0.1 broadcast_select_fusion
  62.9 1.9 %collective-permute-start.7 = (f32[64]{0:T(128)S(1)}, f32[64]{0:T(128)S(1)}, u32[]{:S(2)}, u32[]{:S(2)}) collective-permute-start(f32[64]{0:T(128)S(1)} %broadcast_select_fusion), channel_id=1, source_target_pairs={{0,8},{1,9},{2,10},{3,11},{4,12},{5,13},{6,14},{7,15},{8,0},{9,1},... | collective-permute-start | bytes 776 | tf_op jit(solution)/shard_map/ppermute | solution.py:8
  64.8 0.0 collective-permute-done.6
  64.8 4.9 %all-reduce = f32[128]{0:T(128)S(1)} all-reduce(f32[128]{0:T(128)S(1)} %fusion.18), channel_id=2, replica_groups=mesh['mp'=2,'dp'=16] {'mp'}, use_global_device_ids=true, to_apply=%region_3.4.clone | all-reduce | flops 128 | bytes 1024
  69.7 0.0 collective-permute-done.7
  69.7 0.6 fusion.24
  (8 shorter events, 0.0 us)
Async XLA Ops:
  0.6 2.2 %copy-start = (bf16[1,64,1024]{2,1,0:T(8,128)(2,1)S(1)}, bf16[1,64,1024]{2,1,0:T(8,128)(2,1)}, u32[]{:S(2)}) copy-start(bf16[1,64,1024]{2,1,0:T(8,128)(2,1)} %param.3) | copy-start | bytes 393220
  10.3 1.5 %collective-permute-start = (bf16[128,1024]{1,0:T(8,128)(2,1)S(1)}, bf16[128,1024]{1,0:T(8,128)(2,1)S(1)}, u32[]{:S(2)}, u32[]{:S(2)}) collective-permute-start(bf16[128,1024]{1,0:T(8,128)(2,1)S(1)} %all_gather.3), channel_id=1, source_target_pairs={{0,1},{1,0},{2,3},{3,2},{4,5},{5,4},{6,7},{7,6},{8,9},{9,8},{10,11... | collective-permute-start | bytes 786440 | tf_op jit(solution)/shard_map/ppermute | solution.py:8
  12.0 14.1 %collective-permute-start.1 = (bf16[256,1024]{1,0:T(8,128)(2,1)S(1)}, bf16[256,1024]{1,0:T(8,128)(2,1)S(1)}, u32[]{:S(2)}, u32[]{:S(2)}) collective-permute-start(bf16[256,1024]{1,0:T(8,128)(2,1)S(1)} %maximum_select_fusion.7), channel_id=1, source_target_pairs={{0,2},{1,3},{2,0},{3,1},{4,6},{5,7},{6,4},{7,5},{8,10},{9,11},{10,... | collective-permute-start | bytes 1572872 | tf_op jit(solution)/shard_map/ppermute | solution.py:8
  26.6 27.3 %collective-permute-start.2 = (bf16[512,1024]{1,0:T(8,128)(2,1)S(1)}, bf16[512,1024]{1,0:T(8,128)(2,1)S(1)}, u32[]{:S(2)}, u32[]{:S(2)}) collective-permute-start(bf16[512,1024]{1,0:T(8,128)(2,1)S(1)} %maximum_select_fusion.6), channel_id=1, source_target_pairs={{0,4},{1,5},{2,6},{3,7},{4,0},{5,1},{6,2},{7,3},{8,12},{9,13},{10,... | collective-permute-start | bytes 3145736 | tf_op jit(solution)/shard_map/ppermute | solution.py:8
  28.4 24.7 %collective-permute-start.3 = (bf16[64,1024]{1,0:T(8,128)(2,1)S(1)}, bf16[64,1024]{1,0:T(8,128)(2,1)S(1)}, u32[]{:S(2)}, u32[]{:S(2)}) collective-permute-start(bf16[64,1024]{1,0:T(8,128)(2,1)S(1)} %get-tuple-element.5), channel_id=1, source_target_pairs={{0,8},{1,9},{2,10},{3,11},{4,12},{5,13},{6,14},{7,15},{8,0},{9,1},... | collective-permute-start | bytes 393224 | tf_op jit(solution)/shard_map/ppermute | solution.py:8
  53.8 6.8 %copy-start.1 = (u32[32]{0:T(128)S(1)}, u32[32]{0:T(128)}, u32[]{:S(2)}) copy-start(u32[32]{0:T(128)} %constant.103) | copy-start | bytes 388
  54.7 4.4 %collective-permute-start.4 = (f32[512]{0:T(512)S(1)}, f32[512]{0:T(512)S(1)}, u32[]{:S(2)}, u32[]{:S(2)}) collective-permute-start(f32[512]{0:T(512)S(1)} %slice_select_fusion), channel_id=1, source_target_pairs={{0,4},{1,5},{2,6},{3,7},{4,0},{5,1},{6,2},{7,3},{8,12},{9,13},{10,... | collective-permute-start | bytes 6152 | tf_op jit(solution)/shard_map/ppermute | solution.py:8
  59.1 3.6 %collective-permute-start.5 = (f32[256]{0:T(256)S(1)}, f32[256]{0:T(256)S(1)}, u32[]{:S(2)}, u32[]{:S(2)}) collective-permute-start(f32[256]{0:T(256)S(1)} %broadcast_select_fusion.2), channel_id=1, source_target_pairs={{0,2},{1,3},{2,0},{3,1},{4,6},{5,7},{6,4},{7,5},{8,10},{9,11},{10,... | collective-permute-start | bytes 3080 | tf_op jit(solution)/shard_map/ppermute | solution.py:8
  62.7 2.1 %collective-permute-start.6 = (f32[128]{0:T(128)S(1)}, f32[128]{0:T(128)S(1)}, u32[]{:S(2)}, u32[]{:S(2)}) collective-permute-start(f32[128]{0:T(128)S(1)} %broadcast_select_fusion.3), channel_id=1, source_target_pairs={{0,1},{1,0},{2,3},{3,2},{4,5},{5,4},{6,7},{7,6},{8,9},{9,8},{10,11... | collective-permute-start | bytes 1544 | tf_op jit(solution)/shard_map/ppermute | solution.py:8
  62.9 6.9 %collective-permute-start.7 = (f32[64]{0:T(128)S(1)}, f32[64]{0:T(128)S(1)}, u32[]{:S(2)}, u32[]{:S(2)}) collective-permute-start(f32[64]{0:T(128)S(1)} %broadcast_select_fusion), channel_id=1, source_target_pairs={{0,8},{1,9},{2,10},{3,11},{4,12},{5,13},{6,14},{7,15},{8,0},{9,1},... | collective-permute-start | bytes 776 | tf_op jit(solution)/shard_map/ppermute | solution.py:8
where the time goes:
time: 70.5 us; the launch traced here: 70.3 us
  waiting for transfers between devices  38.3 us (54%)
  starting transfers between devices  12.7 us (18%)
  blocking collectives  12 us (17%)
  other arithmetic  3.78 us (5%)
  between operations  2.02 us (3%)
  matrix products  0.82 us (1%)
    ppermute x8, waiting for transfers between devices, swapped(): lax.ppermute(array, axis, [(i, i ^ 1 << stride) for i in range(lax.axis_s...  38.3 us
    ppermute x8, starting transfers between devices, swapped(): lax.ppermute(array, axis, [(i, i ^ 1 << stride) for i in range(lax.axis_s...  12.7 us
    all_gather x1, blocking collectives, on_device(): image_rows = lax.all_gather(own_img, 'mp', axis=0, tiled=True)  7.12 us
    unnamed x1, blocking collectives  4.93 us
  transfers between devices with their start and end apart: 8, of which 6 were waited for; matrix products, arithmetic and copies ran while one was open for 1% of the time, Pallas kernels for 0%

commit v1 on v0

v1 whole, which is shorter than its diff:
```python
import functools

import jax
import jax.numpy as jnp
from jax import lax
from jax.experimental import pallas as pl
from jax.experimental.pallas import tpu as pltpu
from jax.sharding import PartitionSpec as P

MESH = pl.DeviceIdType.MESH
F32 = jnp.float32


def normalize(raw):
    wide = raw.astype(F32)
    total = jnp.sum(wide * wide, axis=1, keepdims=True)
    return (wide * lax.rsqrt(total + 1e-06)).astype(jnp.bfloat16)


def lane_sums(values):
    folded = values[:, :128]
    for start in range(128, values.shape[1], 128):
        folded = folded + values[:, start : start + 128]
    return jnp.sum(folded.T, axis=0, keepdims=True)


def flipped(index, mask):
    bit = 1
    while bit <= mask:
        if mask & bit:
            index = index + bit * (1 - 2 * (index // bit % 2))
        bit *= 2
    return index


def kernel(
    groups, run, ring,
    scale_ref, image_ref, text_ref, row_ref, col_ref,
    img_raw, txt_raw, img_n, txt_n, weights_col, row_out, row_in, col_out, col_in,
    local_sem, img_send, img_recv, txt_send, txt_recv, row_send, row_recv, col_send, col_recv,
):
    group = lax.axis_index("mp")
    me = lax.axis_index("dp")
    rows = image_ref.shape[0]
    cols = text_ref.shape[0]
    half = rows // 2
    lane = me % run
    spot = me // run

    def along(step):
        return ((spot + step + ring) % ring) * run + lane

    def remote(src, dst, send, recv, dp, mp=None):
        where = {"dp": dp} if mp is None else {"dp": dp, "mp": mp}
        return pltpu.make_async_remote_copy(
            src_ref=src, dst_ref=dst, send_sem=send, recv_sem=recv,
            device_id=where, device_id_type=MESH,
        )

    load_img = pltpu.make_async_copy(image_ref, img_raw.at[0], local_sem.at[0])
    load_txt = pltpu.make_async_copy(text_ref, txt_raw.at[0], local_sem.at[1])
    load_img.start()
    load_txt.start()

    barrier = pltpu.get_barrier_semaphore()
    greeted = 0
    for step in range(1, ring):
        pl.semaphore_signal(barrier, inc=1, device_id={"dp": along(step)}, device_id_type=MESH)
        greeted += 1
    for k in range(run):
        for m in range(groups):
            if k or m:
                pl.semaphore_signal(
                    barrier, inc=1, device_id_type=MESH,
                    device_id={"dp": flipped(me, k), "mp": (group + m) % groups},
                )
                greeted += 1
    pl.semaphore_wait(barrier, greeted)

    def img_copy(way, step, part):
        held = (ring - (step - 1)) % ring if way == 0 else step - 1
        lands = ring - step if way == 0 else step
        span = pl.ds(part * half, half)
        src = image_ref.at[span] if step == 1 else img_raw.at[held, span]
        return remote(
            src, img_raw.at[lands, span],
            img_send.at[way, step - 1, part], img_recv.at[way, step - 1, part],
            along(1 if way == 0 else -1),
        )

    last = ring // 2
    img_copies = {}
    for step in range(1, last + 1):
        for way in range(2):
            for part in ((0, 1) if way == 0 else (1, 0)):
                if step < last or part == way:
                    img_copies[way, step, part] = img_copy(way, step, part)

    def txt_copy(slot):
        bit = slot & -slot
        held = slot - bit
        src = text_ref if held == 0 else txt_raw.at[held]
        return remote(
            src, txt_raw.at[slot], txt_send.at[slot - 1], txt_recv.at[slot - 1],
            flipped(me, bit),
        )

    txt_copies = {slot: txt_copy(slot) for slot in range(1, run)}

    for key in img_copies:
        if key[1] == 1:
            img_copies[key].start()
    for slot in reversed(range(1, run)):
        if slot & (slot - 1) == 0:
            txt_copies[slot].start()

    scale = scale_ref[0]
    load_img.wait()
    load_txt.wait()
    img_n[0] = normalize(img_raw[0])
    txt_n[pl.ds(0, cols)] = normalize(txt_raw[0])
    own = txt_n[pl.ds(pl.multiple_of(group * rows, rows), rows)]
    diag = scale * lane_sums(img_n[0].astype(F32) * own.astype(F32))

    def img_arrive(way, step, part):
        img_copies[way, step, part].wait_recv()
        if (way, step + 1, part) in img_copies:
            img_copies[way, step + 1, part].start()

    for step in range(1, last):
        for order in range(2):
            for way in range(2):
                img_arrive(way, step, way if order == 0 else 1 - way)
        for slot in (step, ring - step):
            img_n[slot] = normalize(img_raw[slot])

    for bit in reversed(range(run.bit_length() - 1)):
        for slot in range(1, run):
            if slot & -slot == 1 << bit:
                txt_copies[slot].wait_recv()
                for low in range(bit):
                    txt_copies[slot + (1 << low)].start()
                txt_n[pl.ds(slot * cols, cols)] = normalize(txt_raw[slot])
    for way in range(2):
        img_arrive(way, last, way)
    img_n[last] = normalize(img_raw[last])

    order = [0]
    for step in range(1, last):
        order += [step, ring - step]
    order.append(last)
    row_copies = []
    for turn, slot in enumerate(order):
        scores = scale * lax.dot_general(
            img_n[slot], txt_n[...], (((1,), (1,)), ((), ())), preferred_element_type=F32
        )
        weights = jnp.exp(scores)
        sums = lane_sums(weights)
        if slot == 0:
            row_in[0, :, :rows] = jnp.broadcast_to(sums, (8, rows))
        else:
            row_out[slot, :, :rows] = jnp.broadcast_to(sums, (8, rows))
            copy = remote(
                row_out.at[slot], row_in.at[ring - slot],
                row_send.at[slot - 1], row_recv.at[ring - slot - 1], along(slot),
            )
            copy.start()
            row_copies.append(copy)
        part = jnp.sum(weights, axis=0, keepdims=True)
        weights_col[...] = part if turn == 0 else weights_col[...] + part

    col_copies = []
    for k in range(run):
        col_out[k] = jnp.broadcast_to(weights_col[:, k * cols : (k + 1) * cols], (8, cols))
        for m in range(groups):
            if k or m:
                copy = remote(
                    col_out.at[k], col_in.at[k * groups + (groups - m) % groups],
                    col_send.at[k * groups + m], col_recv.at[k * groups + (groups - m) % groups],
                    flipped(me, k), (group + m) % groups,
                )
                copy.start()
                col_copies.append(copy)
    row_total = row_in[0, :1, :rows]
    for copy in row_copies:
        copy.wait_recv()
    for slot in range(1, ring):
        row_total = row_total + row_in[slot, :1, :rows]
    row_ref[...] = jnp.log(row_total) - diag
    for copy in col_copies:
        copy.wait_recv()
    col_total = col_out[0, :1]
    for slot in range(1, run * groups):
        col_total = col_total + col_in[slot, :1]
    col_own = col_total[:, :rows]
    for g in range(1, groups):
        col_own = jnp.where(group == g, col_total[:, g * rows : (g + 1) * rows], col_own)
    col_ref[...] = jnp.log(col_own) - diag
    for copy in [*img_copies.values(), *txt_copies.values(), *row_copies, *col_copies]:
        copy.wait_send()


def solution(mesh):
    groups, n = mesh.shape["mp"], mesh.shape["dp"]
    run = 1 << ((n.bit_length() - 1) // 2)
    ring = n // run

    def on_device(image, text, logit_scale):
        _, rows, depth = image.shape
        cols = text.shape[0]
        vmem = pl.BlockSpec(memory_space=pltpu.VMEM)
        hbm = pl.BlockSpec(memory_space=pl.ANY)
        dma = pltpu.SemaphoreType.DMA
        out = jax.ShapeDtypeStruct((1, rows), F32)
        return pl.pallas_call(
            functools.partial(kernel, groups, run, ring),
            out_shape=(out, out),
            in_specs=[pl.BlockSpec(memory_space=pltpu.SMEM), hbm, hbm],
            out_specs=(vmem, vmem),
            scratch_shapes=[
                pltpu.VMEM((ring, rows, depth), jnp.bfloat16),
                pltpu.VMEM((run, cols, depth), jnp.bfloat16),
                pltpu.VMEM((ring, rows, depth), jnp.bfloat16),
                pltpu.VMEM((run * cols, depth), jnp.bfloat16),
                pltpu.VMEM((1, run * cols), F32),
                pltpu.VMEM((ring, 8, 128), F32),
                pltpu.VMEM((ring, 8, 128), F32),
                pltpu.VMEM((run, 8, cols), F32),
                pltpu.VMEM((run * groups, 8, cols), F32),
                dma((2,)),
                dma((2, ring // 2, 2)),
                dma((2, ring // 2, 2)),
                dma((run - 1,)),
                dma((run - 1,)),
                dma((ring - 1,)),
                dma((ring - 1,)),
                dma((run * groups,)),
                dma((run * groups,)),
            ],
            compiler_params=pltpu.CompilerParams(collective_id=0, has_side_effects=True),
        )(logit_scale, image.reshape(rows, depth), text)

    return jax.shard_map(
        on_device,
        mesh=mesh,
        in_specs=(P("dp", "mp", None), P("dp", None), P()),
        out_specs=(P("dp", "mp"), P("dp", "mp")),
        check_vma=False,
    )
```

time: 70.5 us -> 25.9 us (0.37)
  waiting for transfers between devices: 38.3 us -> 0 us
  Pallas kernels: 0 us -> 22.6 us
  starting transfers between devices: 12.7 us -> 0 us
  blocking collectives: 12 us -> 0 us
  other arithmetic: 3.78 us -> 0 us
  local copies, waits for them, and re-layouts: 0.67 us -> 1.8 us
  matrix products: 0.82 us -> 0 us
  between operations: 2.02 us -> 1.29 us
    ppermute x8 -> x0, waiting for transfers between devices: 38.3 us -> none  [swapped(): lax.ppermute(array, axis, [(i, i ^ 1 << stride) for i in range(lax.axis_s...]
    pallas_call x0 -> x1, Pallas kernels: none -> 22.6 us  [on_device(): pl.pallas_call(functools.partial(kernel, groups, run, ring), out_shape=(o...]
    ppermute x8 -> x0, starting transfers between devices: 12.7 us -> none  [swapped(): lax.ppermute(array, axis, [(i, i ^ 1 << stride) for i in range(lax.axis_s...]
    all_gather x1 -> x0, blocking collectives: 7.12 us -> none  [on_device(): image_rows = lax.all_gather(own_img, 'mp', axis=0, tiled=True)]
    unnamed x1 -> x0, blocking collectives: 4.93 us -> none
    reduce_sum x3 -> x0, other arithmetic: 1.46 us -> none  [the longest x2 1.25 us: normalize(): jnp.sum(wide * wide, axis=1, keepdims=True) + 1e-06]
    unnamed x5 -> x6, local copies, waits for them, and re-layouts: 0.59 us -> 1.8 us
    convert_element_type x1 -> x0, other arithmetic: 0.99 us -> none  [normalize(): wide = rows.astype(jnp.float32)]
  transfers between devices with their start and end apart: 8 -> 0, of which waited for: 6 -> 0; matrix products, arithmetic and copies ran while one was open for 1% -> 0% of each run, Pallas kernels for 0% -> 0%
where the time goes in v1:
time: 25.9 us; the launch traced here: 25.7 us
  Pallas kernels  22.6 us (87%)
  local copies, waits for them, and re-layouts  1.8 us (7%)
  between operations  1.29 us (5%)
    pallas_call x1, Pallas kernels, on_device(): pl.pallas_call(functools.partial(kernel, groups, run, ring), out_shape=(o...  22.6 us
    unnamed x6, local copies, waits for them, and re-layouts  1.8 us

profile of v1, /device:TPU:0, one launch (start us, length us, event | category | flops | bytes accessed | tf_op | source)
XLA Modules:
  0.0 25.7 jit_solution(6843636625650859426)
XLA Ops:
  1.3 22.6 %shard_map.50 = (f32[1,64]{1,0:T(1,128)}, f32[1,64]{1,0:T(1,128)}) custom-call(f32[1]{0:T(128)S(6)} %copy.7.scale_ref, bf16[64,1024]{1,0:T(8,128)(2,1)} %bitcast.1, bf16[128,1024]{1,0:T(8,128)(2,1)} %text_ref.1), custom_call_target="tpu_custom_call" | custom-call | tf_op jit(solution)/shard_map/pallas_call | solution.py:215
  23.9 0.0 copy-start.1
  23.9 0.7 %copy-done.1 = f32[1,64]{1,0:T(1,128)S(1)} copy-done((f32[1,64]{1,0:T(1,128)S(1)}, f32[1,64]{1,0:T(1,128)}, u32[]{:S(2)}) %copy-start.1) | copy-done | bytes 280
  24.6 0.0 copy-start
  24.6 0.5 %copy.8 = f32[1,64]{1,0:T(1,128)} copy(f32[1,64]{1,0:T(1,128)S(1)} %copy-done.1) | data formatting | bytes 512
  25.1 0.1 copy-done
  25.2 0.5 %copy.9 = f32[1,64]{1,0:T(1,128)} copy(f32[1,64]{1,0:T(1,128)S(1)} %copy-done) | data formatting | bytes 512
Async XLA Ops:
  23.9 0.7 %copy-start.1 = (f32[1,64]{1,0:T(1,128)S(1)}, f32[1,64]{1,0:T(1,128)}, u32[]{:S(2)}) copy-start(f32[1,64]{1,0:T(1,128)} %get-tuple-element.4) | copy-start | bytes 772
  24.6 0.6 %copy-start = (f32[1,64]{1,0:T(1,128)S(1)}, f32[1,64]{1,0:T(1,128)}, u32[]{:S(2)}) copy-start(f32[1,64]{1,0:T(1,128)} %get-tuple-element.5) | copy-start | bytes 772

commit v2 on v1

v2 whole, which is shorter than its diff:
```python
import functools

import jax
import jax.numpy as jnp
from jax import lax
from jax.experimental import pallas as pl
from jax.experimental.pallas import tpu as pltpu
from jax.sharding import PartitionSpec as P

MESH = pl.DeviceIdType.MESH
F32 = jnp.float32
IMG_PARTS = 4
TXT_PARTS = 2


def normalize(raw):
    wide = raw.astype(F32)
    total = jnp.sum(wide * wide, axis=1, keepdims=True)
    return (wide * lax.rsqrt(total + 1e-06)).astype(jnp.bfloat16)


def lane_sums(values):
    folded = values[:, :128]
    for start in range(128, values.shape[1], 128):
        folded = folded + values[:, start : start + 128]
    return jnp.sum(folded.T, axis=0, keepdims=True)


def low_bit(slot):
    return slot & -slot


def by_level(slots):
    return sorted((s for s in slots if s), key=lambda s: (-low_bit(s), s))


def kernel(
    groups, txt_bits, img_bits,
    scale_ref, image_ref, text_ref, out_ref,
    img_raw, txt_raw, img_n, txt_n, weights_col, row_out, row_in, col_out, col_in,
    local_sem, img_send, img_recv, own_send, own_recv, hop_send, hop_recv,
    mp_send, mp_recv, core_send, core_recv, row_send, row_recv, col_send, col_recv,
):
    group = lax.axis_index("mp")
    me = lax.axis_index("dp")
    rows = image_ref.shape[0]
    cols = text_ref.shape[0]
    n_img, n_txt = 1 << len(img_bits), 1 << len(txt_bits)

    def peer(slot, bits):
        place = me
        for i, bit in enumerate(bits):
            if slot >> i & 1:
                place = place + (1 - 2 * (me // (1 << bit) % 2)) * (1 << bit)
        return place

    def other(m):
        return (group + m) % groups

    def remote(src, dst, send, recv, dp=None, mp=None):
        where = {}
        if dp is not None:
            where["dp"] = dp
        if mp is not None:
            where["mp"] = mp
        return pltpu.make_async_remote_copy(
            src_ref=src, dst_ref=dst, send_sem=send, recv_sem=recv,
            device_id=where, device_id_type=MESH,
        )

    load_img = pltpu.make_async_copy(image_ref, img_raw.at[0], local_sem.at[0])
    load_txt = pltpu.make_async_copy(text_ref, txt_raw.at[0], local_sem.at[1])
    load_img.start()
    load_txt.start()

    barrier = pltpu.get_barrier_semaphore()
    greeted = 0
    for slot in range(1, n_img):
        pl.semaphore_signal(
            barrier, inc=1, device_id={"dp": peer(slot, img_bits)}, device_id_type=MESH
        )
        greeted += 1
    for slot in range(n_txt):
        for m in range(groups):
            if slot or m:
                pl.semaphore_signal(
                    barrier, inc=1, device_id_type=MESH,
                    device_id={"dp": peer(slot, txt_bits), "mp": other(m)},
                )
                greeted += 1
    pl.semaphore_wait(barrier, greeted)
    sent = []

    def start(copy):
        copy.start()
        sent.append(copy)

    img_chunk = rows // IMG_PARTS
    txt_chunk = rows // TXT_PARTS

    def img_copy(slot, part):
        span = pl.ds(part * img_chunk, img_chunk)
        held = slot - low_bit(slot)
        src = img_raw.at[held, span] if held else image_ref.at[span]
        return remote(
            src, img_raw.at[slot, span],
            img_send.at[slot - 1, part], img_recv.at[slot - 1, part],
            peer(low_bit(slot), img_bits),
        )

    def piece(m, part):
        first = (group - m + groups) % groups * rows + part * txt_chunk
        return pl.ds(pl.multiple_of(first, txt_chunk), txt_chunk)

    def hop_copy(slot, part):
        held = slot - low_bit(slot)
        span = piece(0, part)
        src = txt_raw.at[held, span] if held else text_ref.at[span]
        return remote(
            src, txt_raw.at[slot, span],
            hop_send.at[slot, part], hop_recv.at[slot, part],
            peer(low_bit(slot), txt_bits),
        )

    def mp_copy(slot, m, part):
        span = piece(0, part)
        return remote(
            txt_raw.at[slot, span], txt_raw.at[slot, span],
            mp_send.at[slot, m, part], mp_recv.at[slot, m, part], mp=other(m),
        )

    def core_copy(slot, m, part):
        span = piece(m, part)
        return remote(
            txt_raw.at[slot, span], txt_raw.at[slot + 1, span],
            core_send.at[slot, m, part], core_recv.at[slot, m, part], peer(1, txt_bits),
        )

    own_copy = remote(
        text_ref, txt_raw.at[1], own_send.at[0], own_recv.at[0], peer(1, txt_bits)
    )
    even = by_level(range(0, n_txt, 2))
    img_order = by_level(range(n_img))

    for slot in even:
        if slot == low_bit(slot):
            for part in range(TXT_PARTS):
                start(hop_copy(slot, part))
    for slot in img_order:
        if slot == low_bit(slot):
            for part in range(IMG_PARTS):
                start(img_copy(slot, part))
    start(own_copy)

    scale = scale_ref[0]
    load_img.wait()
    load_txt.wait()
    img_n[0] = normalize(img_raw[0])
    txt_n[pl.ds(0, cols)] = normalize(txt_raw[0])
    own = txt_n[pl.ds(pl.multiple_of(group * rows, rows), rows)]
    diag = scale * lane_sums(img_n[0].astype(F32) * own.astype(F32))
    own_copy.wait_recv()
    txt_n[pl.ds(cols, cols)] = normalize(txt_raw[1])

    def text_block(slot):
        txt_n[pl.ds(slot * cols, cols)] = normalize(txt_raw[slot])

    for slot in even:
        for part in range(TXT_PARTS):
            hop_copy(slot, part).wait_recv()
            bit = 2
            while bit < low_bit(slot):
                start(hop_copy(slot + bit, part))
                bit *= 2
            for m in range(1, groups):
                start(mp_copy(slot, m, part))
            start(core_copy(slot, 0, part))

    def img_arrive(slot, part):
        img_copy(slot, part).wait_recv()
        bit = 1
        while bit < low_bit(slot):
            start(img_copy(slot + bit, part))
            bit *= 2

    def img_block(slot):
        img_n[slot] = normalize(img_raw[slot])

    final = img_order[-1]
    early = [s for s in img_order if s == 1]
    passed = [s for s in img_order if s not in early and s != final]
    text_waits = [(slot, m, part) for slot in even for part in range(TXT_PARTS) for m in range(1, groups)]
    image_waits = [(slot, part) for slot in passed for part in range(IMG_PARTS)]
    for slot in early:
        for part in range(IMG_PARTS):
            img_arrive(slot, part)
        if slot != final:
            img_block(slot)
    share = -(-len(image_waits) // max(len(text_waits), 1))
    for i in range(max(len(text_waits), 1)):
        for slot, m, part in text_waits[i : i + 1]:
            mp_copy(slot, m, part).wait_recv()
            start(core_copy(slot, m, part))
        for slot, part in image_waits[i * share : (i + 1) * share]:
            img_arrive(slot, part)
    for slot in even:
        text_block(slot)
    for slot in passed:
        img_block(slot)
    for slot in even:
        for m in range(groups):
            for part in range(TXT_PARTS):
                core_copy(slot, m, part).wait_recv()
        text_block(slot + 1)

    row_copies = []

    def image_rows(slot, first):
        scores = scale * lax.dot_general(
            img_n[slot], txt_n[...], (((1,), (1,)), ((), ())), preferred_element_type=F32
        )
        weights = jnp.exp(scores)
        sums = jnp.broadcast_to(lane_sums(weights), (8, rows))
        if slot == 0:
            row_in[0, :, :rows] = sums
        else:
            row_out[slot, :, :rows] = sums
            copy = remote(
                row_out.at[slot], row_in.at[slot],
                row_send.at[slot - 1], row_recv.at[slot - 1], peer(slot, img_bits),
            )
            start(copy)
            row_copies.append(copy)
        part = jnp.sum(weights, axis=0, keepdims=True)
        weights_col[...] = part if first else weights_col[...] + part

    for slot in [0, *early, *passed]:
        if slot != final:
            image_rows(slot, slot == 0)
    if final not in early:
        for part in range(IMG_PARTS):
            img_arrive(final, part)
    img_block(final)
    image_rows(final, False)

    col_copies = []
    for slot in range(n_txt):
        col_out[slot] = jnp.broadcast_to(
            weights_col[:, slot * cols : (slot + 1) * cols], (8, cols)
        )
        for m in range(groups):
            if slot or m:
                to = slot * groups + (groups - m) % groups
                copy = remote(
                    col_out.at[slot], col_in.at[to],
                    col_send.at[slot * groups + m], col_recv.at[to],
                    peer(slot, txt_bits), other(m),
                )
                start(copy)
                col_copies.append(copy)
    row_total = row_in[0, :1, :rows]
    for copy in row_copies:
        copy.wait_recv()
    for slot in range(1, n_img):
        row_total = row_total + row_in[slot, :1, :rows]
    for copy in col_copies:
        copy.wait_recv()
    col_total = col_out[0, :1]
    for slot in range(1, n_txt * groups):
        col_total = col_total + col_in[slot, :1]
    col_own = col_total[:, :rows]
    for g in range(1, groups):
        col_own = jnp.where(group == g, col_total[:, g * rows : (g + 1) * rows], col_own)
    out_ref[0:1] = row_total
    out_ref[1:2] = col_own
    out_ref[2:3] = diag
    for copy in sent:
        copy.wait_send()


def solution(mesh):
    groups, n = mesh.shape["mp"], mesh.shape["dp"]
    levels = n.bit_length() - 1
    txt_bits = list(range(0, levels, 2))
    img_bits = list(range(1, levels, 2))
    n_txt, n_img = 1 << len(txt_bits), 1 << len(img_bits)

    def on_device(image, text, logit_scale):
        _, rows, depth = image.shape
        cols = text.shape[0]
        hbm = pl.BlockSpec(memory_space=pl.ANY)
        dma = pltpu.SemaphoreType.DMA
        totals = pl.pallas_call(
            functools.partial(kernel, groups, txt_bits, img_bits),
            out_shape=jax.ShapeDtypeStruct((3, rows), F32),
            in_specs=[pl.BlockSpec(memory_space=pltpu.SMEM), hbm, hbm],
            out_specs=pl.BlockSpec(memory_space=pltpu.VMEM),
            scratch_shapes=[
                pltpu.VMEM((n_img, rows, depth), jnp.bfloat16),
                pltpu.VMEM((n_txt, cols, depth), jnp.bfloat16),
                pltpu.VMEM((n_img, rows, depth), jnp.bfloat16),
                pltpu.VMEM((n_txt * cols, depth), jnp.bfloat16),
                pltpu.VMEM((1, n_txt * cols), F32),
                pltpu.VMEM((n_img, 8, 128), F32),
                pltpu.VMEM((n_img, 8, 128), F32),
                pltpu.VMEM((n_txt, 8, cols), F32),
                pltpu.VMEM((n_txt * groups, 8, cols), F32),
                dma((2,)),
                dma((n_img - 1, IMG_PARTS)),
                dma((n_img - 1, IMG_PARTS)),
                dma((1,)),
                dma((1,)),
                dma((n_txt, TXT_PARTS)),
                dma((n_txt, TXT_PARTS)),
                dma((n_txt, groups, TXT_PARTS)),
                dma((n_txt, groups, TXT_PARTS)),
                dma((n_txt, groups, TXT_PARTS)),
                dma((n_txt, groups, TXT_PARTS)),
                dma((n_img - 1,)),
                dma((n_img - 1,)),
                dma((n_txt * groups,)),
                dma((n_txt * groups,)),
            ],
            compiler_params=pltpu.CompilerParams(collective_id=0, has_side_effects=True),
        )(logit_scale, image.reshape(rows, depth), text)
        row_loss = jnp.log(totals[0:1]) - totals[2:3]
        col_loss = jnp.log(totals[1:2]) - totals[2:3]
        return (row_loss, col_loss)

    return jax.shard_map(
        on_device,
        mesh=mesh,
        in_specs=(P("dp", "mp", None), P("dp", None), P()),
        out_specs=(P("dp", "mp"), P("dp", "mp")),
        check_vma=False,
    )
```

time: 25.9 us -> 26.8 us (1.035)
  local copies, waits for them, and re-layouts: 1.8 us -> 0 us
  Pallas kernels: 22.6 us -> 24.1 us
  other arithmetic: 0 us -> 1.31 us
    unnamed x6 -> x0, local copies, waits for them, and re-layouts: 1.8 us -> none
    pallas_call x1, Pallas kernels: 22.6 us -> 24.1 us  [on_device(): pl.pallas_call(functools.partial(kernel, groups, txt_bits, img_bits), out...]
    sub x0 -> x1, other arithmetic: none -> 1.31 us  [on_device(): col_loss = jnp.log(totals[1:2]) - totals[2:3]]
where the time goes in v2:
time: 26.8 us; the launch traced here: 26.7 us
  Pallas kernels  24.1 us (90%)
  other arithmetic  1.31 us (5%)
  between operations  1.28 us (5%)
    pallas_call x1, Pallas kernels, on_device(): pl.pallas_call(functools.partial(kernel, groups, txt_bits, img_bits), out...  24.1 us
    sub x1, other arithmetic, on_device(): col_loss = jnp.log(totals[1:2]) - totals[2:3]  1.31 us

profile of v2, /device:TPU:0, one launch (start us, length us, event | category | flops | bytes accessed | tf_op | source)
XLA Modules:
  0.0 26.7 jit_solution(17623215515584132)
XLA Ops:
  1.3 24.1 %shard_map.50 = f32[3,64]{1,0:T(4,128)} custom-call(f32[1]{0:T(128)S(6)} %copy.5.scale_ref, bf16[64,1024]{1,0:T(8,128)(2,1)} %bitcast.1, bf16[128,1024]{1,0:T(8,128)(2,1)} %text_ref.1), custom_call_target="tpu_custom_call" | custom-call | tf_op jit(solution)/shard_map/pallas_call | solution.py:293
  25.4 1.3 %log_subtract_fusion = (f32[1,64]{1,0:T(1,128)}, f32[1,64]{1,0:T(1,128)}) fusion(f32[3,64]{1,0:T(4,128)} %shard_map.50), kind=kLoop, calls=%fused_computation | loop fusion | flops 128 | bytes 1280 | tf_op jit(solution)/shard_map/sub | solution.py:327

commit v3 on v1

v3 whole, which is shorter than its diff:
```python
import functools

import jax
import jax.numpy as jnp
from jax import lax
from jax.experimental import pallas as pl
from jax.experimental.pallas import tpu as pltpu
from jax.sharding import PartitionSpec as P

MESH = pl.DeviceIdType.MESH
F32 = jnp.float32
IMG_PARTS = 4
TXT_PARTS = 2


def normalize(raw):
    wide = raw.astype(F32)
    total = jnp.sum(wide * wide, axis=1, keepdims=True)
    return (wide * lax.rsqrt(total + 1e-06)).astype(jnp.bfloat16)


def lane_sums(values):
    folded = values[:, :128]
    for start in range(128, values.shape[1], 128):
        folded = folded + values[:, start : start + 128]
    return jnp.sum(folded.T, axis=0, keepdims=True)


def flipped(index, mask):
    bit = 1
    while bit <= mask:
        if mask & bit:
            index = index + bit * (1 - 2 * (index // bit % 2))
        bit *= 2
    return index


def kernel(
    groups, run, ring,
    scale_ref, image_ref, text_ref, out_ref,
    image_own, img_raw, txt_raw, img_n, txt_n, weights_col, row_out, row_in, col_out, col_in,
    local_sem, img_send, img_recv, txt_send, txt_recv, row_send, row_recv, col_send, col_recv,
):
    group = lax.axis_index("mp")
    me = lax.axis_index("dp")
    rows = image_ref.shape[0]
    cols = text_ref.shape[0]
    lane = me % run
    spot = me // run

    def along(step):
        return ((spot + step + ring) % ring) * run + lane

    def remote(src, dst, send, recv, dp, mp=None):
        where = {"dp": dp} if mp is None else {"dp": dp, "mp": mp}
        return pltpu.make_async_remote_copy(
            src_ref=src, dst_ref=dst, send_sem=send, recv_sem=recv,
            device_id=where, device_id_type=MESH,
        )

    load_img = pltpu.make_async_copy(image_ref, image_own, local_sem.at[0])
    load_txt = pltpu.make_async_copy(text_ref, txt_raw.at[0], local_sem.at[1])
    load_img.start()
    load_txt.start()

    barrier = pltpu.get_barrier_semaphore()
    greeted = 0
    for step in range(1, ring):
        pl.semaphore_signal(barrier, inc=1, device_id={"dp": along(step)}, device_id_type=MESH)
        greeted += 1
    for k in range(run):
        for m in range(groups):
            if k or m:
                pl.semaphore_signal(
                    barrier, inc=1, device_id_type=MESH,
                    device_id={"dp": flipped(me, k), "mp": (group + m) % groups},
                )
                greeted += 1
    pl.semaphore_wait(barrier, greeted)

    part_rows = rows // IMG_PARTS
    img_sent = []

    def img_copy(way, source, part, own=False):
        span = pl.ds(part * part_rows, part_rows)
        return remote(
            image_ref.at[span] if own else img_raw.at[source, span],
            img_raw.at[source, span],
            img_send.at[way, source, part], img_recv.at[source, part],
            along(1 - 2 * way),
        )

    def pass_on(source, part, own=False):
        for way in range(2):
            if own:
                goes = spot < ring - 1 if way == 0 else spot > 0
            elif way == 0:
                goes = jnp.logical_and(source < spot, spot < ring - 1)
            else:
                goes = jnp.logical_and(source > spot, spot > 0)
            copy = img_copy(way, source, part, own)
            img_sent.append((goes, copy))

            @pl.when(goes)
            def _():
                copy.start()

    short = jnp.minimum(spot, ring - 1 - spot)
    ahead = jnp.where(spot < ring - 1 - spot, 1, -1)

    def nearest(turn):
        both = (turn + 1) // 2 * (1 - 2 * (turn % 2))
        return spot + jnp.where(turn <= 2 * short, both, ahead * (turn - short))

    txt_rows = cols // TXT_PARTS

    def txt_copy(slot, part):
        bit = slot & -slot
        held = slot - bit
        span = pl.ds(part * txt_rows, txt_rows)
        return remote(
            txt_raw.at[held, span] if held else text_ref.at[span],
            txt_raw.at[slot, span],
            txt_send.at[slot - 1, part], txt_recv.at[slot - 1, part], flipped(me, bit),
        )

    txt_sent = []

    def txt_start(slot, part):
        copy = txt_copy(slot, part)
        copy.start()
        txt_sent.append(copy)

    def txt_arrive(slot, part):
        txt_copy(slot, part).wait_recv()
        bit = 1
        while bit < slot & -slot:
            txt_start(slot + bit, part)
            bit *= 2

    def txt_block(slot):
        txt_n[pl.ds(slot * cols, cols)] = normalize(txt_raw[slot])

    for part in range(IMG_PARTS):
        pass_on(spot, part, True)
    for slot in reversed(range(1, run)):
        if slot & (slot - 1) == 0:
            for part in range(TXT_PARTS):
                txt_start(slot, part)

    scale = scale_ref[0]
    load_img.wait()
    load_txt.wait()
    img_n[0] = normalize(image_own[...])
    txt_n[pl.ds(0, cols)] = normalize(txt_raw[0])
    own = txt_n[pl.ds(pl.multiple_of(group * rows, rows), rows)]
    diag = scale * lane_sums(img_n[0].astype(F32) * own.astype(F32))

    def img_arrive(turn, part):
        source = nearest(turn)
        img_copy(0, source, part).wait_recv()
        pass_on(source, part)

    def img_block(turn):
        img_n[turn] = normalize(img_raw[nearest(turn)])

    txt_order = sorted(range(1, run), key=lambda k: -(k & -k))
    txt_waits = [(slot, part) for slot in txt_order if slot % 2 == 0 for part in range(TXT_PARTS)]
    img_waits = [(turn, part) for turn in range(1, ring - 1) for part in range(IMG_PARTS)]
    lead = min(IMG_PARTS, len(img_waits))
    for turn, part in img_waits[:lead]:
        img_arrive(turn, part)
    rest = img_waits[lead:]
    share = -(-len(rest) // max(len(txt_waits), 1))
    for i in range(max(len(txt_waits), 1)):
        for slot, part in txt_waits[i : i + 1]:
            txt_arrive(slot, part)
        for turn, part in rest[i * share : (i + 1) * share]:
            img_arrive(turn, part)
    for slot in txt_order:
        if slot % 2 == 0:
            txt_block(slot)
    for turn in range(1, ring - 1):
        img_block(turn)
    for slot in txt_order:
        if slot % 2:
            for part in range(TXT_PARTS):
                txt_arrive(slot, part)
            txt_block(slot)

    row_copies = []

    def image_rows(turn):
        scores = scale * lax.dot_general(
            img_n[turn], txt_n[...], (((1,), (1,)), ((), ())), preferred_element_type=F32
        )
        weights = jnp.exp(scores)
        sums = jnp.broadcast_to(lane_sums(weights), (8, rows))
        if turn == 0:
            row_in[spot, :, :rows] = sums
        else:
            row_out[turn, :, :rows] = sums
            copy = remote(
                row_out.at[turn], row_in.at[spot],
                row_send.at[turn - 1], row_recv.at[spot],
                nearest(turn) * run + lane,
            )
            copy.start()
            row_copies.append(copy)
        part = jnp.sum(weights, axis=0, keepdims=True)
        weights_col[...] = part if turn == 0 else weights_col[...] + part

    for turn in range(ring - 1):
        image_rows(turn)
    for part in range(IMG_PARTS):
        img_arrive(ring - 1, part)
    img_block(ring - 1)
    image_rows(ring - 1)

    col_copies = []
    for k in range(run):
        col_out[k] = jnp.broadcast_to(weights_col[:, k * cols : (k + 1) * cols], (8, cols))
        for m in range(groups):
            if k or m:
                to = k * groups + (groups - m) % groups
                copy = remote(
                    col_out.at[k], col_in.at[to],
                    col_send.at[k * groups + m], col_recv.at[to],
                    flipped(me, k), (group + m) % groups,
                )
                copy.start()
                col_copies.append(copy)
    for turn in range(1, ring):
        source = nearest(turn)
        remote(
            row_out.at[turn], row_in.at[source], row_send.at[turn - 1], row_recv.at[source],
            source * run + lane,
        ).wait_recv()
    row_total = row_in[0, :1, :rows]
    for slot in range(1, ring):
        row_total = row_total + row_in[slot, :1, :rows]
    for copy in col_copies:
        copy.wait_recv()
    col_total = col_out[0, :1]
    for slot in range(1, run * groups):
        col_total = col_total + col_in[slot, :1]
    col_own = col_total[:, :rows]
    for g in range(1, groups):
        col_own = jnp.where(group == g, col_total[:, g * rows : (g + 1) * rows], col_own)
    out_ref[0:1] = row_total
    out_ref[1:2] = col_own
    out_ref[2:3] = diag
    for goes, copy in img_sent:

        @pl.when(goes)
        def _():
            copy.wait_send()

    for copy in [*txt_sent, *row_copies, *col_copies]:
        copy.wait_send()


def solution(mesh):
    groups, n = mesh.shape["mp"], mesh.shape["dp"]
    run = 1 << ((n.bit_length() - 1) // 2)
    ring = n // run

    def on_device(image, text, logit_scale):
        _, rows, depth = image.shape
        cols = text.shape[0]
        hbm = pl.BlockSpec(memory_space=pl.ANY)
        dma = pltpu.SemaphoreType.DMA
        totals = pl.pallas_call(
            functools.partial(kernel, groups, run, ring),
            out_shape=jax.ShapeDtypeStruct((3, rows), F32),
            in_specs=[pl.BlockSpec(memory_space=pltpu.SMEM), hbm, hbm],
            out_specs=pl.BlockSpec(memory_space=pltpu.VMEM),
            scratch_shapes=[
                pltpu.VMEM((rows, depth), jnp.bfloat16),
                pltpu.VMEM((ring, rows, depth), jnp.bfloat16),
                pltpu.VMEM((run, cols, depth), jnp.bfloat16),
                pltpu.VMEM((ring, rows, depth), jnp.bfloat16),
                pltpu.VMEM((run * cols, depth), jnp.bfloat16),
                pltpu.VMEM((1, run * cols), F32),
                pltpu.VMEM((ring, 8, 128), F32),
                pltpu.VMEM((ring, 8, 128), F32),
                pltpu.VMEM((run, 8, cols), F32),
                pltpu.VMEM((run * groups, 8, cols), F32),
                dma((2,)),
                dma((2, ring, IMG_PARTS)),
                dma((ring, IMG_PARTS)),
                dma((run - 1, TXT_PARTS)),
                dma((run - 1, TXT_PARTS)),
                dma((ring - 1,)),
                dma((ring,)),
                dma((run * groups,)),
                dma((run * groups,)),
            ],
            compiler_params=pltpu.CompilerParams(collective_id=0, has_side_effects=True),
        )(logit_scale, image.reshape(rows, depth), text)
        row_loss = jnp.log(totals[0:1]) - totals[2:3]
        col_loss = jnp.log(totals[1:2]) - totals[2:3]
        return (row_loss, col_loss)

    return jax.shard_map(
        on_device,
        mesh=mesh,
        in_specs=(P("dp", "mp", None), P("dp", None), P()),
        out_specs=(P("dp", "mp"), P("dp", "mp")),
        check_vma=False,
    )
```

time: 25.9 us -> 27.9 us (1.077)
  Pallas kernels: 22.6 us -> 25.2 us
  local copies, waits for them, and re-layouts: 1.8 us -> 0 us
  other arithmetic: 0 us -> 1.31 us
    pallas_call x1, Pallas kernels: 22.6 us -> 25.2 us  [on_device(): pl.pallas_call(functools.partial(kernel, groups, run, ring), out_shape=ja...]
    unnamed x6 -> x0, local copies, waits for them, and re-layouts: 1.8 us -> none
    sub x0 -> x1, other arithmetic: none -> 1.31 us  [on_device(): col_loss = jnp.log(totals[1:2]) - totals[2:3]]
where the time goes in v3:
time: 27.9 us; the launch traced here: 27.7 us
  Pallas kernels  25.2 us (90%)
  other arithmetic  1.31 us (5%)
  between operations  1.28 us (5%)
    pallas_call x1, Pallas kernels, on_device(): pl.pallas_call(functools.partial(kernel, groups, run, ring), out_shape=ja...  25.2 us
    sub x1, other arithmetic, on_device(): col_loss = jnp.log(totals[1:2]) - totals[2:3]  1.31 us

profile of v3, /device:TPU:0, one launch (start us, length us, event | category | flops | bytes accessed | tf_op | source)
XLA Modules:
  0.0 27.7 jit_solution(11408150180549869274)
XLA Ops:
  1.3 25.2 %shard_map.50 = f32[3,64]{1,0:T(4,128)} custom-call(f32[1]{0:T(128)S(6)} %copy.5.scale_ref, bf16[64,1024]{1,0:T(8,128)(2,1)} %bitcast.1, bf16[128,1024]{1,0:T(8,128)(2,1)} %text_ref.1), custom_call_target="tpu_custom_call" | custom-call | tf_op jit(solution)/shard_map/pallas_call | solution.py:273
  26.4 1.3 %log_subtract_fusion = (f32[1,64]{1,0:T(1,128)}, f32[1,64]{1,0:T(1,128)}) fusion(f32[3,64]{1,0:T(4,128)} %shard_map.50), kind=kLoop, calls=%fused_computation | loop fusion | flops 128 | bytes 1280 | tf_op jit(solution)/shard_map/sub | solution.py:302

commit v4 on v3

--- a/solution.py
+++ b/solution.py
@@ -79,7 +79,6 @@
     pl.semaphore_wait(barrier, greeted)
 
     part_rows = rows // IMG_PARTS
-    img_sent = []
 
     def img_copy(way, source, part, own=False):
         span = pl.ds(part * part_rows, part_rows)
@@ -90,7 +89,7 @@
             along(1 - 2 * way),
         )
 
-    def pass_on(source, part, own=False):
+    def pass_on(source, part, own=False, ended=False):
         for way in range(2):
             if own:
                 goes = spot < ring - 1 if way == 0 else spot > 0
@@ -99,11 +98,10 @@
             else:
                 goes = jnp.logical_and(source > spot, spot > 0)
             copy = img_copy(way, source, part, own)
-            img_sent.append((goes, copy))
 
             @pl.when(goes)
             def _():
-                copy.start()
+                copy.wait_send() if ended else copy.start()
 
     short = jnp.minimum(spot, ring - 1 - spot)
     ahead = jnp.where(spot < ring - 1 - spot, 1, -1)
@@ -166,17 +164,33 @@
 
     txt_order = sorted(range(1, run), key=lambda k: -(k & -k))
     txt_waits = [(slot, part) for slot in txt_order if slot % 2 == 0 for part in range(TXT_PARTS)]
-    img_waits = [(turn, part) for turn in range(1, ring - 1) for part in range(IMG_PARTS)]
-    lead = min(IMG_PARTS, len(img_waits))
+    img_waits = [
+        (turn, part)
+        for pair in range(1, ring, 2)
+        for part in range(IMG_PARTS)
+        for turn in range(pair, min(pair + 2, ring))
+    ]
+    at_end = jnp.logical_or(spot == 0, spot == ring - 1)
+
+    def img_early(turn, part):
+        if turn < ring - 1:
+            img_arrive(turn, part)
+        else:
+
+            @pl.when(jnp.logical_not(at_end))
+            def _():
+                img_arrive(turn, part)
+
+    lead = min(2 * IMG_PARTS, len(img_waits))
     for turn, part in img_waits[:lead]:
-        img_arrive(turn, part)
+        img_early(turn, part)
     rest = img_waits[lead:]
-    share = -(-len(rest) // max(len(txt_waits), 1))
+    share = -(-len(rest) // max(len(txt_waits) - 1, 1))
     for i in range(max(len(txt_waits), 1)):
         for slot, part in txt_waits[i : i + 1]:
             txt_arrive(slot, part)
         for turn, part in rest[i * share : (i + 1) * share]:
-            img_arrive(turn, part)
+            img_early(turn, part)
     for slot in txt_order:
         if slot % 2 == 0:
             txt_block(slot)
@@ -213,7 +227,11 @@
     for turn in range(ring - 1):
         image_rows(turn)
     for part in range(IMG_PARTS):
-        img_arrive(ring - 1, part)
+
+        @pl.when(at_end)
+        def _():
+            img_copy(0, nearest(ring - 1), part).wait_recv()
+
     img_block(ring - 1)
     image_rows(ring - 1)
 
@@ -250,12 +268,10 @@
     out_ref[0:1] = row_total
     out_ref[1:2] = col_own
     out_ref[2:3] = diag
-    for goes, copy in img_sent:
-
-        @pl.when(goes)
-        def _():
-            copy.wait_send()
-
+    for part in range(IMG_PARTS):
+        pass_on(spot, part, True, True)
+        for turn in range(1, ring):
+            pass_on(nearest(turn), part, False, True)
     for copy in [*txt_sent, *row_copies, *col_copies]:
         copy.wait_send()
 

time: 27.9 us -> 25.2 us (0.903)
  Pallas kernels: 25.2 us -> 22.5 us
    pallas_call x1, Pallas kernels: 25.2 us -> 22.5 us  [on_device(): pl.pallas_call(functools.partial(kernel, groups, run, ring), out_shape=ja...]
where the time goes in v4:
time: 25.2 us; the launch traced here: 25 us
  Pallas kernels  22.5 us (89%)
  other arithmetic  1.31 us (5%)
  between operations  1.28 us (5%)
    pallas_call x1, Pallas kernels, on_device(): pl.pallas_call(functools.partial(kernel, groups, run, ring), out_shape=ja...  22.5 us
    sub x1, other arithmetic, on_device(): col_loss = jnp.log(totals[1:2]) - totals[2:3]  1.31 us

profile of v4, /device:TPU:0, one launch (start us, length us, event | category | flops | bytes accessed | tf_op | source)
XLA Modules:
  0.0 25.0 jit_solution(9719100731450374631)
XLA Ops:
  1.3 22.5 %shard_map.50 = f32[3,64]{1,0:T(4,128)} custom-call(f32[1]{0:T(128)S(6)} %copy.5.scale_ref, bf16[64,1024]{1,0:T(8,128)(2,1)} %bitcast.1, bf16[128,1024]{1,0:T(8,128)(2,1)} %text_ref.1), custom_call_target="tpu_custom_call" | custom-call | tf_op jit(solution)/shard_map/pallas_call | solution.py:289
  23.7 1.3 %log_subtract_fusion = (f32[1,64]{1,0:T(1,128)}, f32[1,64]{1,0:T(1,128)}) fusion(f32[3,64]{1,0:T(4,128)} %shard_map.50), kind=kLoop, calls=%fused_computation | loop fusion | flops 128 | bytes 1280 | tf_op jit(solution)/shard_map/sub | solution.py:318

commit v5 on v1

--- a/solution.py
+++ b/solution.py
@@ -35,7 +35,7 @@
 
 def kernel(
     groups, run, ring,
-    scale_ref, image_ref, text_ref, row_ref, col_ref,
+    scale_ref, image_ref, text_ref, out_ref,
     img_raw, txt_raw, img_n, txt_n, weights_col, row_out, row_in, col_out, col_in,
     local_sem, img_send, img_recv, txt_send, txt_recv, row_send, row_recv, col_send, col_recv,
 ):
@@ -141,9 +141,6 @@
                 for low in range(bit):
                     txt_copies[slot + (1 << low)].start()
                 txt_n[pl.ds(slot * cols, cols)] = normalize(txt_raw[slot])
-    for way in range(2):
-        img_arrive(way, last, way)
-    img_n[last] = normalize(img_raw[last])
 
     order = [0]
     for step in range(1, last):
@@ -151,6 +148,10 @@
     order.append(last)
     row_copies = []
     for turn, slot in enumerate(order):
+        if slot == last:
+            for way in range(2):
+                img_arrive(way, last, way)
+            img_n[last] = normalize(img_raw[last])
         scores = scale * lax.dot_general(
             img_n[slot], txt_n[...], (((1,), (1,)), ((), ())), preferred_element_type=F32
         )
@@ -186,7 +187,8 @@
         copy.wait_recv()
     for slot in range(1, ring):
         row_total = row_total + row_in[slot, :1, :rows]
-    row_ref[...] = jnp.log(row_total) - diag
+    out_ref[0:1] = row_total
+    out_ref[2:3] = diag
     for copy in col_copies:
         copy.wait_recv()
     col_total = col_out[0, :1]
@@ -195,7 +197,7 @@
     col_own = col_total[:, :rows]
     for g in range(1, groups):
         col_own = jnp.where(group == g, col_total[:, g * rows : (g + 1) * rows], col_own)
-    col_ref[...] = jnp.log(col_own) - diag
+    out_ref[1:2] = col_own
     for copy in [*img_copies.values(), *txt_copies.values(), *row_copies, *col_copies]:
         copy.wait_send()
 
@@ -211,12 +213,11 @@
         vmem = pl.BlockSpec(memory_space=pltpu.VMEM)
         hbm = pl.BlockSpec(memory_space=pl.ANY)
         dma = pltpu.SemaphoreType.DMA
-        out = jax.ShapeDtypeStruct((1, rows), F32)
-        return pl.pallas_call(
+        totals = pl.pallas_call(
             functools.partial(kernel, groups, run, ring),
-            out_shape=(out, out),
+            out_shape=jax.ShapeDtypeStruct((3, rows), F32),
             in_specs=[pl.BlockSpec(memory_space=pltpu.SMEM), hbm, hbm],
-            out_specs=(vmem, vmem),
+            out_specs=vmem,
             scratch_shapes=[
                 pltpu.VMEM((ring, rows, depth), jnp.bfloat16),
                 pltpu.VMEM((run, cols, depth), jnp.bfloat16),
@@ -239,6 +240,9 @@
             ],
             compiler_params=pltpu.CompilerParams(collective_id=0, has_side_effects=True),
         )(logit_scale, image.reshape(rows, depth), text)
+        row_loss = jnp.log(totals[0:1]) - totals[2:3]
+        col_loss = jnp.log(totals[1:2]) - totals[2:3]
+        return (row_loss, col_loss)
 
     return jax.shard_map(
         on_device,

time: 25.9 us -> 24.3 us (0.938)
  local copies, waits for them, and re-layouts: 1.8 us -> 0 us
  other arithmetic: 0 us -> 1.31 us
  Pallas kernels: 22.6 us -> 21.6 us
    unnamed x6 -> x0, local copies, waits for them, and re-layouts: 1.8 us -> none
    sub x0 -> x1, other arithmetic: none -> 1.31 us  [on_device(): col_loss = jnp.log(totals[1:2]) - totals[2:3]]
    pallas_call x1, Pallas kernels: 22.6 us -> 21.6 us  [on_device(): pl.pallas_call(functools.partial(kernel, groups, run, ring), out_shape=ja...]
where the time goes in v5:
time: 24.3 us; the launch traced here: 24.1 us
  Pallas kernels  21.6 us (89%)
  other arithmetic  1.31 us (5%)
  between operations  1.28 us (5%)
    pallas_call x1, Pallas kernels, on_device(): pl.pallas_call(functools.partial(kernel, groups, run, ring), out_shape=ja...  21.6 us
    sub x1, other arithmetic, on_device(): col_loss = jnp.log(totals[1:2]) - totals[2:3]  1.31 us

profile of v5, /device:TPU:0, one launch (start us, length us, event | category | flops | bytes accessed | tf_op | source)
XLA Modules:
  0.0 24.1 jit_solution(2675386498847305875)
XLA Ops:
  1.3 21.6 %shard_map.50 = f32[3,64]{1,0:T(4,128)} custom-call(f32[1]{0:T(128)S(6)} %copy.5.scale_ref, bf16[64,1024]{1,0:T(8,128)(2,1)} %bitcast.1, bf16[128,1024]{1,0:T(8,128)(2,1)} %text_ref.1), custom_call_target="tpu_custom_call" | custom-call | tf_op jit(solution)/shard_map/pallas_call | solution.py:216
  22.8 1.3 %log_subtract_fusion = (f32[1,64]{1,0:T(1,128)}, f32[1,64]{1,0:T(1,128)}) fusion(f32[3,64]{1,0:T(4,128)} %shard_map.50), kind=kLoop, calls=%fused_computation | loop fusion | flops 128 | bytes 1280 | tf_op jit(solution)/shard_map/sub | solution.py:244

commit v6 on v4

--- a/solution.py
+++ b/solution.py
@@ -9,8 +9,8 @@
 
 MESH = pl.DeviceIdType.MESH
 F32 = jnp.float32
-IMG_PARTS = 4
-TXT_PARTS = 2
+IMG_PARTS = 2
+TXT_PARTS = 1
 
 
 def normalize(raw):
@@ -181,16 +181,30 @@
             def _():
                 img_arrive(turn, part)
 
-    lead = min(2 * IMG_PARTS, len(img_waits))
-    for turn, part in img_waits[:lead]:
-        img_early(turn, part)
-    rest = img_waits[lead:]
-    share = -(-len(rest) // max(len(txt_waits) - 1, 1))
-    for i in range(max(len(txt_waits), 1)):
-        for slot, part in txt_waits[i : i + 1]:
-            txt_arrive(slot, part)
-        for turn, part in rest[i * share : (i + 1) * share]:
-            img_early(turn, part)
+    for turn, part in img_waits[: 2 * IMG_PARTS]:
+        if turn == 1:
+            img_arrive(turn, part)
+        else:
+
+            @pl.when(jnp.logical_not(at_end))
+            def _():
+                img_arrive(turn, part)
+
+    for turn, part in img_waits[2 * IMG_PARTS :]:
+
+        @pl.when(jnp.logical_not(at_end))
+        def _():
+            img_arrive(turn, part)
+
+    for slot, part in txt_waits:
+        txt_arrive(slot, part)
+    for turn, part in img_waits:
+        if 1 < turn < ring - 1:
+
+            @pl.when(at_end)
+            def _():
+                img_arrive(turn, part)
+
     for slot in txt_order:
         if slot % 2 == 0:
             txt_block(slot)
@@ -204,11 +218,14 @@
 
     row_copies = []
 
-    def image_rows(turn):
+    def image_weights(first, count):
+        block = img_n[pl.ds(first, count)].reshape(count * rows, -1)
         scores = scale * lax.dot_general(
-            img_n[turn], txt_n[...], (((1,), (1,)), ((), ())), preferred_element_type=F32
+            block, txt_n[...], (((1,), (1,)), ((), ())), preferred_element_type=F32
         )
-        weights = jnp.exp(scores)
+        return jnp.exp(scores)
+
+    def image_rows(turn, weights):
         sums = jnp.broadcast_to(lane_sums(weights), (8, rows))
         if turn == 0:
             row_in[spot, :, :rows] = sums
@@ -224,8 +241,9 @@
         part = jnp.sum(weights, axis=0, keepdims=True)
         weights_col[...] = part if turn == 0 else weights_col[...] + part
 
+    early = image_weights(0, ring - 1)
     for turn in range(ring - 1):
-        image_rows(turn)
+        image_rows(turn, early[turn * rows : (turn + 1) * rows])
     for part in range(IMG_PARTS):
 
         @pl.when(at_end)
@@ -233,7 +251,7 @@
             img_copy(0, nearest(ring - 1), part).wait_recv()
 
     img_block(ring - 1)
-    image_rows(ring - 1)
+    image_rows(ring - 1, image_weights(ring - 1, 1))
 
     col_copies = []
     for k in range(run):

time: 25.2 us -> 24.3 us (0.964)
  Pallas kernels: 22.5 us -> 21.6 us
    pallas_call x1, Pallas kernels: 22.5 us -> 21.6 us  [on_device(): pl.pallas_call(functools.partial(kernel, groups, run, ring), out_shape=ja...]
where the time goes in v6:
time: 24.3 us; the launch traced here: 24.2 us
  Pallas kernels  21.6 us (89%)
  other arithmetic  1.31 us (5%)
  between operations  1.28 us (5%)
    pallas_call x1, Pallas kernels, on_device(): pl.pallas_call(functools.partial(kernel, groups, run, ring), out_shape=ja...  21.6 us
    sub x1, other arithmetic, on_device(): col_loss = jnp.log(totals[1:2]) - totals[2:3]  1.31 us

profile of v6, /device:TPU:0, one launch (start us, length us, event | category | flops | bytes accessed | tf_op | source)
XLA Modules:
  0.0 24.2 jit_solution(17297988275014108900)
XLA Ops:
  1.3 21.6 %shard_map.50 = f32[3,64]{1,0:T(4,128)} custom-call(f32[1]{0:T(128)S(6)} %copy.5.scale_ref, bf16[64,1024]{1,0:T(8,128)(2,1)} %bitcast.1, bf16[128,1024]{1,0:T(8,128)(2,1)} %text_ref.1), custom_call_target="tpu_custom_call" | custom-call | tf_op jit(solution)/shard_map/pallas_call | solution.py:307
  22.9 1.3 %log_subtract_fusion = (f32[1,64]{1,0:T(1,128)}, f32[1,64]{1,0:T(1,128)}) fusion(f32[3,64]{1,0:T(4,128)} %shard_map.50), kind=kLoop, calls=%fused_computation | loop fusion | flops 128 | bytes 1280 | tf_op jit(solution)/shard_map/sub | solution.py:336
